TPU v7x, 256 devices: a whole 4x4x8 slice. The times are simulated.
256 devices in a mesh: row: 32 (over z, y_lo, core), col: 8 (over y_hi, x).
Axes of the slice: x: 4, y: 4 (y_hi: 2, y_lo: 2; y = y_hi * 2 + y_lo), z: 8, core: 2. Of those that a mesh axis runs over, the one named last changes fastest.
Arguments:
- features: bfloat16 [32768, 128], P(('col', 'row')), may hold values from -96 to 96
- weight: bfloat16 [128, 256], replicated, may hold values from -0.5 to 0.5
- bias: float32 [256], replicated, may hold values from -3 to 3
- cotangent: bfloat16 [32768, 256], P(('row', 'col')), may hold values from -6 to 6
- tile_values: bfloat16 [32, 8, 256, 128, 128], P('row', 'col'), may hold values from 0 to 4, as said below
- tile_pos: int32 [32, 8, 2, 256], P('row', 'col'), may hold values from 0 to 31, as said below
- tile_count: int32 [32, 8], P('row', 'col'), may hold values from 0 to 256, as said below
- block_perm: int32 [256], replicated, may hold values from 0 to 255, as said below
Outputs:
- hidden: bfloat16 [32768, 256], P(('row', 'col'))
- weight_grad: float32 [128, 256], replicated
- bias_grad: float32 [256], replicated
Inputs may be any that keep to these rules, and one draw needn't show every extreme that they name: `tile_values`: entries are 0 or a weight of at least 0.25; slots t at or beyond tile_count[r, c] belong to no tile. `tile_pos`: entry [r, c, 0, t] is the slot's tile row, below 8, within row block r, and [r, c, 1, t] its tile column, below 32, within column block c, both in the reordered numbering; the slots of one cell hold distinct positions. `tile_count`: every draw has a cell with 256 live slots. `block_perm`: each aligned run of 8 entries is a permutation of that run's own indices.
All inputs are finite; a program needn't handle non-finite values.
Results may differ from a plain program's by a relative error of at most 0.0059.
Values may be sent and summed in bfloat16 or wider, within the bound.
No kernel may reach another device: no remote copies, remote signals or barrier semaphores. Data moves between devices by JAX's collectives and lax.ppermute only.
A program may use at most 64 MiB of HBM per device.

v0:
```python
import jax
import jax.numpy as jnp
from jax import lax
from jax.sharding import PartitionSpec as P


def local_index(block_perm, tile_axis, block_index, run_length):
    return jnp.take(block_perm, block_index * run_length + tile_axis) - block_index * run_length


def body(features, weight, bias, cotangent, tile_values, tile_pos, tile_count, block_perm):
    row_count = lax.axis_size("row")
    col_count = lax.axis_size("col")
    row_index = lax.axis_index("row")
    col_index = lax.axis_index("col")
    packed = tile_values[0, 0]
    positions = tile_pos[0, 0]
    live_count = tile_count[0, 0]
    max_tiles = packed.shape[0]
    tile_size = packed.shape[1]
    feat_width = features.shape[1]
    row_tiles = block_perm.shape[0] // row_count
    col_tiles = row_tiles * row_count // col_count
    block_tiles = min(64, max_tiles)
    lane_index = jnp.arange(block_tiles, dtype=jnp.int32)
    own_rows = local_index(block_perm, positions[0], row_index, row_tiles)
    own_cols = local_index(block_perm, positions[1], col_index, col_tiles)

    def degree_step(block_step, totals):
        row_acc, col_acc = totals
        slot_number = block_step * block_tiles + lane_index
        is_live = slot_number < live_count
        clamped = jnp.minimum(slot_number, max_tiles - 1)
        values = jnp.take(packed, clamped, axis=0).astype(jnp.float32)
        row_part = jnp.sum(values, axis=2)
        col_part = jnp.sum(values, axis=1)
        row_part = jnp.where(is_live[:, None], row_part, 0.0)
        col_part = jnp.where(is_live[:, None], col_part, 0.0)
        row_acc = row_acc.at[jnp.take(own_rows, clamped)].add(row_part)
        col_acc = col_acc.at[jnp.take(own_cols, clamped)].add(col_part)
        return (row_acc, col_acc)

    degree_blocks = (live_count + block_tiles - 1) // block_tiles
    row_acc, col_acc = lax.fori_loop(
        jnp.int32(0),
        degree_blocks,
        degree_step,
        (
            jnp.zeros((row_tiles, tile_size), jnp.float32),
            jnp.zeros((col_tiles, tile_size), jnp.float32),
        ),
    )
    col_part_flat = col_acc.reshape(col_tiles * tile_size)
    col_share = lax.psum_scatter(col_part_flat, "row", scatter_dimension=0, tiled=True)
    scaled = (lax.rsqrt(1.0 + col_share)[:, None] * features.astype(jnp.float32)).astype(
        jnp.bfloat16
    )
    gathered = lax.all_gather(scaled, "row", axis=0, tiled=True)
    feature_tiles = gathered.reshape(col_tiles, tile_size, feat_width)
    list_length = packed.shape[0]

    def product_step(block_step, partial_value):
        logical = block_step * block_tiles + lane_index
        is_live = logical < live_count
        is_upper = logical >= live_count
        source = jnp.where(is_upper, logical - live_count, logical)
        source = jnp.clip(source, 0, list_length - 1)
        slot_number = jnp.minimum(is_upper.astype(jnp.int32), 1 - 1)
        tile_block = jnp.take(packed, source, axis=0)
        tile_block = jnp.where(is_live[:, None, None], tile_block, jnp.zeros((), jnp.bfloat16))
        inputs = jnp.take(feature_tiles, jnp.take(own_cols, source), axis=0)
        products = jnp.einsum(
            "bpq,bqf->bpf", tile_block, inputs, preferred_element_type=jnp.float32
        )
        return partial_value.at[slot_number, jnp.take(own_rows, source)].add(products)

    product_blocks = (live_count + block_tiles - 1) // block_tiles
    initial = jnp.zeros((1, row_tiles, tile_size, feat_width), jnp.float32)
    partial_value = lax.fori_loop(jnp.int32(0), product_blocks, product_step, initial)
    own_sum = partial_value[0]
    row_part_flat = row_acc.reshape(row_tiles * tile_size)
    summed, degree_share = (
        lax.psum_scatter(
            own_sum.reshape(row_tiles * tile_size, feat_width),
            "col",
            scatter_dimension=0,
            tiled=True,
        ),
        lax.psum_scatter(row_part_flat, "col", scatter_dimension=0, tiled=True),
    )
    aggregated = (lax.rsqrt(1.0 + degree_share)[:, None] * summed).astype(jnp.bfloat16)
    preact = jnp.dot(aggregated, weight, preferred_element_type=jnp.float32) + bias
    logistic = jax.nn.sigmoid(preact)
    hidden = (preact * logistic).astype(jnp.bfloat16)
    preact_grad = (
        cotangent.astype(jnp.float32) * logistic * (1.0 + preact * (1.0 - logistic))
    ).astype(jnp.bfloat16)
    weight_part = jnp.einsum(
        "nf,nh->fh", aggregated, preact_grad, preferred_element_type=jnp.float32
    )
    bias_part = jnp.sum(preact_grad.astype(jnp.float32), axis=0)
    weight_sum, bias_sum = lax.psum((weight_part, bias_part), ("row", "col"))
    inverse_root = lax.rsqrt(jnp.float32(summed.shape[0] * row_count * col_count))
    return (hidden, weight_sum * inverse_root, bias_sum * inverse_root)


def solution(mesh):
    placed = (
        P(("col", "row"), None),
        P(),
        P(),
        P(("row", "col"), None),
        P("row", "col", None, None, None),
        P("row", "col", None, None),
        P("row", "col"),
        P(),
    )
    return jax.shard_map(
        body,
        mesh=mesh,
        in_specs=placed,
        out_specs=(P(("row", "col"), None), P(), P()),
        check_vma=False,
    )
```

profile of v0, /device:TPU:2, one launch (start us, length us, event | category | flops | bytes accessed | tf_op | source)
XLA Modules:
  0.0 723.7 jit_solution(14614431443404107920)
XLA Ops:
  8.7 2.0 gather_fusion.8
  10.7 2.0 gather_fusion.7
  12.7 9.5 %while.24 = (s32[]{:T(128)}, f32[8,128]{1,0:T(8,128)S(1)}, f32[32,128]{1,0:T(8,128)S(1)}, s32[]{:T(128)}, s32[256]{0:T(256)S(1)}, /*index=5*/s32[]{:T(128)}, bf1...) while((s32[]{:T(128)}, f32[8,128]{1,0:T(8,128)S(1)}, ...), condition=%wide.region_5.9_spmd.clone, body=%wide.region_0.8_spmd.clone.sunk | while | flops 4213635 | bytes 6451793 | solution.py:44
  13.4 0.8 gather_fusion.1
  14.2 0.8 gather_fusion
  15.0 4.3 gather_fusion.2
  19.4 0.9 convert_reduce_fusion.4
  20.2 1.0 scatter_custom_fusion.15
  21.2 1.0 scatter_custom_fusion.16
  22.2 122.7 %all-reduce.1 = f32[4096]{0:T(1024)S(1)} all-reduce(f32[4096]{0:T(1024)S(1)} %bitcast.44), channel_id=3, replica_groups=mesh['row'=32,'col'=8] {'row'}, use_global_device_ids=true, to_apply=%region_7.11.clone | all-reduce | flops 4096 | bytes 32768
  147.1 74.5 %all-gather.2.cloned.1.call-done = bf16[4096,128]{1,0:T(8,128)(2,1)} async-done(((bf16[128,128]{1,0:T(8,128)(2,1)}), bf16[4096,128]{1,0:T(8,128)(2,1)}) %all-gather.2.cloned.1.call-update) | async-done | bytes 1048592 | tf_op jit(solution)/shard_map/all_gather | solution.py:58
  221.6 24.0 %while.25 = (s32[]{:T(128)}, f32[1,8,128,128]{3,2,1,0:T(8,128)S(1)}, s32[]{:T(128)}, s32[]{:T(128)}, s32[256]{0:T(256)S(1)}, /*index=5*/bf16[256,128,128]{2,1,0:...) while((s32[]{:T(128)}, f32[1,8,128,128]{3,2,1,0:T(8,128)S(1)}, ...), condition=%wide.region_10.14_spmd.clone, body=%wide.region_8.13_spmd.clone.sunk | while | flops 272634240 | bytes 41956408 | solution.py:79
  223.2 0.8 gather_fusion.3
  224.7 2.2 gather_fusion.6
  226.8 5.7 gather_fusion.4
  232.5 4.3 fusion.45
  236.8 8.8 %scatter_fusion = f32[8,128,128]{2,1,0:T(8,128)S(1)} fusion(f32[8,128,128]{2,1,0:T(8,128)S(1)} %bitcast.39, s32[64]{0:T(128)S(1)} %fusion.44, f32[64,128,128]{2,1,0:T(8,128)} %fusion.45), kind=kCustom, calls=%fused_computation.11.clone.clone.1 | custom fusion | flops 1048576 | bytes 12583168 | tf_op jit(solution)/shard_map/while/body/scatter-add | solution.py:75
  247.7 43.6 %all-reduce = f32[1024]{0:T(1024)S(1)} all-reduce(f32[1024]{0:T(1024)S(1)} %bitcast.45), channel_id=2, replica_groups=mesh['row'=32,'col'=8] {'col'}, use_global_device_ids=true, to_apply=%region_6.10.clone | all-reduce | flops 1024 | bytes 8192
  291.4 102.7 %reduce-scatter.2.cloned.1.call-done = f32[128,128]{1,0:T(8,128)} async-done(((f32[1024,128]{1,0:T(8,128)}), f32[128,128]{1,0:T(8,128)}) %reduce-scatter.2.cloned.1.call-update) | async-done | bytes 65552 | tf_op jit(solution)/shard_map/reduce_scatter | solution.py:83
  394.1 1.7 convert_reduce_fusion.2
  395.8 73.9 %psum.15 = f32[256]{0:T(256)S(1)} all-reduce(f32[256]{0:T(256)S(1)} %get-tuple-element.182), channel_id=1, replica_groups=mesh['row'=32,'col'=8] {'row','col'}, use_global_device_ids=true, to_apply=%region_14.18 | all-reduce | flops 256 | bytes 2048 | tf_op jit(solution)/shard_map/psum | solution.py:102
  469.8 1.8 fusion.33
  472.1 243.5 %all-reduce.4.cloned.1.call-done = f32[128,256]{1,0:T(8,128)} async-done(((f32[128,256]{1,0:T(8,128)}), f32[128,256]{1,0:T(8,128)}) %all-reduce.4.cloned.1.call-update) | async-done | bytes 131088 | tf_op jit(solution)/shard_map/psum | solution.py:102
  715.6 1.6 broadcast_multiply_fusion
  (49 shorter events, 7.3 us)
Async XLA Ops:
  7.2 386.9 %copy-start = (bf16[128,256]{1,0:T(8,128)(2,1)S(1)}, bf16[128,256]{1,0:T(8,128)(2,1)}, u32[]{:S(2)}) copy-start(bf16[128,256]{1,0:T(8,128)(2,1)} %param.19) | copy-start | bytes 196612
  7.2 214.3 %all-gather.2.cloned.1.call-start = ((), (), s32[]{:S(2)}) async-start(), calls=%async_computation.1 | async-start | bytes 1081344 | tf_op jit(solution)/shard_map/all_gather | solution.py:58
  12.7 132.3 %copy-start.8 = (u32[256]{0:T(256)S(1)}, u32[256]{0:T(256)}, u32[]{:S(2)}) copy-start(u32[256]{0:T(256)} %constant.133) | copy-start | bytes 3076
  12.7 133.6 %copy-start.4 = (bf16[128,128]{1,0:T(8,128)(2,1)S(1)}, bf16[128,128]{1,0:T(8,128)(2,1)}, u32[]{:S(2)}) copy-start(bf16[128,128]{1,0:T(8,128)(2,1)} %param.18) | copy-start | bytes 98308
  12.7 381.4 %copy-start.5 = (bf16[128,256]{1,0:T(8,128)(2,1)S(1)}, bf16[128,256]{1,0:T(8,128)(2,1)}, u32[]{:S(2)}) copy-start(bf16[128,256]{1,0:T(8,128)(2,1)} %param.21) | copy-start | bytes 196612
  147.0 247.1 %reduce-scatter.2.cloned.1.call-start = ((), (), s32[]{:S(2)}) async-start(), calls=%async_computation.2 | async-start | bytes 589824 | tf_op jit(solution)/shard_map/reduce_scatter | solution.py:83
  221.6 24.9 %copy-start.7 = (u32[256]{0:T(256)S(1)}, u32[256]{0:T(256)}, u32[]{:S(2)}) copy-start(u32[256]{0:T(256)} %constant.129) | copy-start | bytes 3076
  221.6 172.5 %copy-start.6 = (f32[256]{0:T(256)S(1)}, f32[256]{0:T(256)}, u32[]{:S(2)}) copy-start(f32[256]{0:T(256)} %param.20) | copy-start | bytes 3076
  221.6 3.1 copy-start.2
  226.8 5.7 copy-start.3
  245.6 0.8 copy-start.1
  246.4 469.2 %all-reduce.4.cloned.1.call-start = ((), (), s32[]{:S(2)}) async-start(), calls=%async_computation.3 | async-start | bytes 262144 | tf_op jit(solution)/shard_map/psum | solution.py:102
Sparse Core Ops, SparseCore 0:
  147.1 74.3 all-gather.1
  246.6 147.4 reduce-scatter.1
  471.7 243.8 all-reduce.3
where the time goes:
time: 725 us; the launch traced here: 724 us
  waiting for transfers between devices  421 us (58%)
  blocking collectives  240 us (33%)
  local copies, waits for them, and re-layouts  21.3 us (3%)
  other arithmetic  17.5 us (2%)
  between operations  15.9 us (2%)
  matrix products  7.81 us (1%)
    psum x1, waiting for transfers between devices, body(): weight_sum, bias_sum = lax.psum((weight_part, bias_part), ('row', 'col'))  243 us
    unnamed x2, blocking collectives  166 us
    reduce_scatter x1, waiting for transfers between devices, body(): lax.psum_scatter(own_sum.reshape(row_tiles * tile_size, feat_width), 'col...  103 us
    all_gather x1, waiting for transfers between devices, body(): gathered = lax.all_gather(scaled, 'row', axis=0, tiled=True)  74.5 us
    psum x1, blocking collectives, body(): weight_sum, bias_sum = lax.psum((weight_part, bias_part), ('row', 'col'))  73.9 us
  transfers between devices with their start and end apart: 3, of which 3 were waited for; matrix products, arithmetic and copies ran while one was open for 0% of the time, Pallas kernels for 0%

commit v1 on v0

--- a/solution.py
+++ b/solution.py
@@ -2,6 +2,11 @@
 import jax.numpy as jnp
 from jax import lax
 from jax.sharding import PartitionSpec as P
+
+
+def by_each_axis(x, axis_one, axis_two):
+    partial = lax.psum(x, axis_one)
+    return lax.psum(partial, axis_two)
 
 
 def local_index(block_perm, tile_axis, block_index, run_length):
@@ -99,7 +104,7 @@
         "nf,nh->fh", aggregated, preact_grad, preferred_element_type=jnp.float32
     )
     bias_part = jnp.sum(preact_grad.astype(jnp.float32), axis=0)
-    weight_sum, bias_sum = lax.psum((weight_part, bias_part), ("row", "col"))
+    weight_sum, bias_sum = by_each_axis((weight_part, bias_part), "col", "row")
     inverse_root = lax.rsqrt(jnp.float32(summed.shape[0] * row_count * col_count))
     return (hidden, weight_sum * inverse_root, bias_sum * inverse_root)
 

time: 725 us -> 702 us (0.968)
  waiting for transfers between devices: 421 us -> 399 us
    psum x1 -> x2, waiting for transfers between devices: 243 us -> 222 us  [the longest x1 209 us: by_each_axis(): return lax.psum(partial, axis_two)]
    psum x1 -> x2, blocking collectives: 73.9 us -> 72.8 us  [the longest x1 53 us: by_each_axis(): return lax.psum(partial, axis_two)]
  transfers between devices with their start and end apart: 3 -> 4, of which waited for: 3 -> 4; matrix products, arithmetic and copies ran while one was open for 0% -> 0% of each run, Pallas kernels for 0% -> 0%
where the time goes in v1:
time: 702 us; the launch traced here: 701 us
  waiting for transfers between devices  399 us (57%)
  blocking collectives  239 us (34%)
  local copies, waits for them, and re-layouts  21.3 us (3%)
  other arithmetic  17.5 us (2%)
  between operations  15.9 us (2%)
  matrix products  7.81 us (1%)
    psum x1, waiting for transfers between devices, by_each_axis(): return lax.psum(partial, axis_two)  209 us
    unnamed x2, blocking collectives  166 us
    reduce_scatter x1, waiting for transfers between devices, body(): lax.psum_scatter(own_sum.reshape(row_tiles * tile_size, feat_width), 'col...  103 us
    all_gather x1, waiting for transfers between devices, body(): gathered = lax.all_gather(scaled, 'row', axis=0, tiled=True)  74.5 us
    psum x1, blocking collectives, by_each_axis(): return lax.psum(partial, axis_two)  53 us
    psum x1, blocking collectives, by_each_axis(): partial = lax.psum(x, axis_one)  19.8 us
  transfers between devices with their start and end apart: 4, of which 4 were waited for; matrix products, arithmetic and copies ran while one was open for 0% of the time, Pallas kernels for 0%

profile of v1, /device:TPU:2, one launch (start us, length us, event | category | flops | bytes accessed | tf_op | source)
XLA Modules:
  0.0 700.8 jit_solution(10879429908123594634)
XLA Ops:
  8.7 2.0 gather_fusion.8
  10.7 2.0 gather_fusion.7
  12.7 9.5 %while.24 = (s32[]{:T(128)}, f32[8,128]{1,0:T(8,128)S(1)}, f32[32,128]{1,0:T(8,128)S(1)}, s32[]{:T(128)}, s32[256]{0:T(256)S(1)}, /*index=5*/s32[]{:T(128)}, bf1...) while((s32[]{:T(128)}, f32[8,128]{1,0:T(8,128)S(1)}, ...), condition=%wide.region_5.9_spmd.clone, body=%wide.region_0.8_spmd.clone.sunk | while | flops 4213635 | bytes 6451793 | solution.py:49
  14.2 0.8 gather_fusion
  15.0 4.3 gather_fusion.2
  19.4 0.9 convert_reduce_fusion.4
  20.2 1.0 scatter_custom_fusion.15
  21.2 1.0 scatter_custom_fusion.16
  22.2 122.7 %all-reduce.1 = f32[4096]{0:T(1024)S(1)} all-reduce(f32[4096]{0:T(1024)S(1)} %bitcast.44), channel_id=3, replica_groups=mesh['row'=32,'col'=8] {'row'}, use_global_device_ids=true, to_apply=%region_7.11.clone | all-reduce | flops 4096 | bytes 32768
  147.1 74.5 %all-gather.2.cloned.1.call-done = bf16[4096,128]{1,0:T(8,128)(2,1)} async-done(((bf16[128,128]{1,0:T(8,128)(2,1)}), bf16[4096,128]{1,0:T(8,128)(2,1)}) %all-gather.2.cloned.1.call-update) | async-done | bytes 1048592 | tf_op jit(solution)/shard_map/all_gather | solution.py:63
  221.6 24.0 %while.25 = (s32[]{:T(128)}, f32[1,8,128,128]{3,2,1,0:T(8,128)S(1)}, s32[]{:T(128)}, s32[]{:T(128)}, s32[256]{0:T(256)S(1)}, /*index=5*/bf16[256,128,128]{2,1,0:...) while((s32[]{:T(128)}, f32[1,8,128,128]{3,2,1,0:T(8,128)S(1)}, ...), condition=%wide.region_10.14_spmd.clone, body=%wide.region_8.13_spmd.clone.sunk | while | flops 272634240 | bytes 41956408 | solution.py:84
  224.7 2.2 gather_fusion.6
  226.8 5.7 gather_fusion.4
  232.5 4.3 fusion.45
  236.8 8.8 %scatter_fusion = f32[8,128,128]{2,1,0:T(8,128)S(1)} fusion(f32[8,128,128]{2,1,0:T(8,128)S(1)} %bitcast.39, s32[64]{0:T(128)S(1)} %fusion.44, f32[64,128,128]{2,1,0:T(8,128)} %fusion.45), kind=kCustom, calls=%fused_computation.11.clone.clone.1 | custom fusion | flops 1048576 | bytes 12583168 | tf_op jit(solution)/shard_map/while/body/scatter-add | solution.py:80
  247.7 43.6 %all-reduce = f32[1024]{0:T(1024)S(1)} all-reduce(f32[1024]{0:T(1024)S(1)} %bitcast.45), channel_id=2, replica_groups=mesh['row'=32,'col'=8] {'col'}, use_global_device_ids=true, to_apply=%region_6.10.clone | all-reduce | flops 1024 | bytes 8192
  291.4 102.7 %reduce-scatter.2.cloned.1.call-done = f32[128,128]{1,0:T(8,128)} async-done(((f32[1024,128]{1,0:T(8,128)}), f32[128,128]{1,0:T(8,128)}) %reduce-scatter.2.cloned.1.call-update) | async-done | bytes 65552 | tf_op jit(solution)/shard_map/reduce_scatter | solution.py:88
  394.1 1.7 convert_reduce_fusion.2
  395.8 1.8 fusion.33
  397.7 19.8 %psum.30 = f32[256]{0:T(256)S(1)} all-reduce(f32[256]{0:T(256)S(1)} %get-tuple-element.182), channel_id=1, replica_groups=mesh['row'=32,'col'=8] {'col'}, use_global_device_ids=true, to_apply=%region_15.19 | all-reduce | flops 256 | bytes 2048 | tf_op jit(solution)/shard_map/psum | solution.py:8
  417.5 53.0 %psum.31 = f32[256]{0:T(256)S(1)} all-reduce(f32[256]{0:T(256)S(1)} %psum.30), channel_id=1, replica_groups=mesh['row'=32,'col'=8] {'row'}, use_global_device_ids=true, to_apply=%region_16.20 | all-reduce | flops 256 | bytes 2048 | tf_op jit(solution)/shard_map/psum | solution.py:9
  470.4 12.8 %all-reduce.5.cloned.1.call-done = f32[128,256]{1,0:T(8,128)} async-done(((f32[128,256]{1,0:T(8,128)}), f32[128,256]{1,0:T(8,128)}) %all-reduce.5.cloned.1.call-update) | async-done | bytes 131088 | tf_op jit(solution)/shard_map/psum | solution.py:8
  483.8 208.9 %all-reduce.7.cloned.1.call-done = f32[128,256]{1,0:T(8,128)} async-done(((f32[128,256]{1,0:T(8,128)}), f32[128,256]{1,0:T(8,128)}) %all-reduce.7.cloned.1.call-update) | async-done | bytes 131088 | tf_op jit(solution)/shard_map/psum | solution.py:9
  692.7 1.6 broadcast_multiply_fusion
  (53 shorter events, 9.0 us)
Async XLA Ops:
  7.2 386.9 %copy-start = (bf16[128,256]{1,0:T(8,128)(2,1)S(1)}, bf16[128,256]{1,0:T(8,128)(2,1)}, u32[]{:S(2)}) copy-start(bf16[128,256]{1,0:T(8,128)(2,1)} %param.19) | copy-start | bytes 196612
  7.2 214.3 %all-gather.2.cloned.1.call-start = ((), (), s32[]{:S(2)}) async-start(), calls=%async_computation.1 | async-start | bytes 1081344 | tf_op jit(solution)/shard_map/all_gather | solution.py:63
  12.7 132.3 %copy-start.8 = (u32[256]{0:T(256)S(1)}, u32[256]{0:T(256)}, u32[]{:S(2)}) copy-start(u32[256]{0:T(256)} %constant.133) | copy-start | bytes 3076
  12.7 133.6 %copy-start.4 = (bf16[128,128]{1,0:T(8,128)(2,1)S(1)}, bf16[128,128]{1,0:T(8,128)(2,1)}, u32[]{:S(2)}) copy-start(bf16[128,128]{1,0:T(8,128)(2,1)} %param.18) | copy-start | bytes 98308
  12.7 381.4 %copy-start.5 = (bf16[128,256]{1,0:T(8,128)(2,1)S(1)}, bf16[128,256]{1,0:T(8,128)(2,1)}, u32[]{:S(2)}) copy-start(bf16[128,256]{1,0:T(8,128)(2,1)} %param.21) | copy-start | bytes 196612
  147.0 247.1 %reduce-scatter.2.cloned.1.call-start = ((), (), s32[]{:S(2)}) async-start(), calls=%async_computation.2 | async-start | bytes 589824 | tf_op jit(solution)/shard_map/reduce_scatter | solution.py:88
  221.6 24.9 %copy-start.7 = (u32[256]{0:T(256)S(1)}, u32[256]{0:T(256)}, u32[]{:S(2)}) copy-start(u32[256]{0:T(256)} %constant.129) | copy-start | bytes 3076
  221.6 172.5 %copy-start.6 = (f32[256]{0:T(256)S(1)}, f32[256]{0:T(256)}, u32[]{:S(2)}) copy-start(f32[256]{0:T(256)} %param.20) | copy-start | bytes 3076
  221.6 3.1 copy-start.2
  226.8 5.7 copy-start.3
  245.6 0.8 copy-start.1
  246.4 236.8 %all-reduce.5.cloned.1.call-start = ((), (), s32[]{:S(2)}) async-start(), calls=%async_computation.3 | async-start | bytes 262144 | tf_op jit(solution)/shard_map/psum | solution.py:8
  397.6 295.1 %all-reduce.7.cloned.1.call-start = ((), (), s32[]{:S(2)}) async-start(), calls=%async_computation.4 | async-start | bytes 262144 | tf_op jit(solution)/shard_map/psum | solution.py:9
Sparse Core Ops, SparseCore 0:
  147.1 74.3 all-gather.1
  246.6 147.4 reduce-scatter.1
  397.7 85.4 all-reduce.4
  485.7 206.9 all-reduce.6
